TPU v7x, 32 devices: a whole 2x2x4 slice. The times are simulated.
32 devices in a mesh: seq: 16 (over z, y, x), head: 2 (over core).
Axes of the slice: x: 2, y: 2, z: 4, core: 2. Of those that a mesh axis runs over, the one named last changes fastest.
Arguments:
- queries: bfloat16 [2048, 2048], P('seq', 'head'), may hold values from -144 to 144
- keys: bfloat16 [2048, 2048], P('seq', 'head'), may hold values from -4 to 4
- values: bfloat16 [2048, 2048], P('seq', 'head'), may hold values from -6 to 6
- grad_out: bfloat16 [2048, 2048], P('seq', 'head'), may hold values from -6 to 6
- bias_table: float32 [32, 128], P('head'), may hold values from -5 to 5
- bucket_ids: int32 [16, 4, 256], P('seq'), may hold values from 0 to 127
- block_mask: int32 [16, 4], P('seq'), may hold values 0 or 1
Outputs:
- grad_queries: bfloat16 [2048, 2048], P('seq', 'head')
- grad_keys: bfloat16 [2048, 2048], P('seq', 'head')
- grad_values: bfloat16 [2048, 2048], P('seq', 'head')
- grad_bias: float32 [32, 128], replicated
All inputs are finite; a program needn't handle non-finite values. No bound on the sum of `block_mask` on one device may be relied on, other than what follows from the above.
Results may differ from a plain program's by a relative error of at most 0.005.
Values may be sent and summed in bfloat16 or wider, within the bound.
No kernel may reach another device: no remote copies, remote signals or barrier semaphores. Data moves between devices by JAX's collectives and lax.ppermute only.
A program may use at most 64 MiB of HBM per device.

v0:
```python
import jax
import jax.numpy as jnp
from jax import lax
from jax.sharding import PartitionSpec as P


def passed_along(value, axis, by):
    devices = lax.axis_size(axis)
    pairs = [(i, i + by) for i in range(devices) if 0 <= i + by < devices]
    return lax.ppermute(value, axis, pairs)


def diagonal_sums(field):
    heads, rows, _ = field.shape
    flipped = field[:, :, ::-1]
    padded = jnp.pad(flipped, ((0, 0), (0, 0), (0, rows)))
    sheared = padded.reshape(heads, 2 * rows * rows)[:, : rows * (2 * rows - 1)]
    sums = sheared.reshape(heads, rows, 2 * rows - 1).sum(axis=1)
    return jnp.pad(sums, ((0, 0), (0, 1)))


def toeplitz_rows(by_offset, rows):
    heads = by_offset.shape[0]
    reverse = by_offset[:, : 2 * rows - 1][:, ::-1]
    tiled = jnp.tile(reverse, (1, rows))
    window = tiled[:, rows - 1 : rows - 1 + rows * (2 * rows - 2)]
    return window.reshape(heads, rows, 2 * rows - 2)[:, :, :rows]


def body(queries, keys, values, grad_out, bias_table, bucket_ids, block_mask):
    tok, width = queries.shape
    heads, buckets = bias_table.shape
    head_dim = width // heads
    span = block_mask.shape[1]
    scale = head_dim ** (-0.5)
    highest = lax.Precision.HIGHEST
    index = lax.axis_index("seq")
    query_heads = queries.reshape(tok, heads, head_dim)
    cot_heads = grad_out.reshape(tok, heads, head_dim)
    rows = jnp.arange(tok, dtype=jnp.int32)
    lower = rows[:, None] >= rows[None, :]
    codes = jnp.arange(buckets, dtype=jnp.int32)
    table_ids = bucket_ids[0]
    flags = block_mask[0]

    def pair_terms(key_blk, value_blk, step):
        ids = lax.dynamic_index_in_dim(table_ids, step, 0, keepdims=False)
        onehot = (ids[:, None] == codes[None, :]).astype(jnp.float32)
        by_offset = jnp.dot(bias_table, onehot.T, precision=highest)
        bias_full = toeplitz_rows(by_offset, tok)
        key_heads = key_blk.reshape(tok, heads, head_dim)
        value_heads = value_blk.reshape(tok, heads, head_dim)
        scores = (
            scale
            * jnp.einsum("qhd,khd->hqk", query_heads, key_heads, preferred_element_type=jnp.float32)
            + bias_full
        )
        dprob = jnp.einsum(
            "qhd,khd->hqk", cot_heads, value_heads, preferred_element_type=jnp.float32
        )
        flag = lax.dynamic_index_in_dim(flags, step, 0, keepdims=False)
        whole = (flag == 1) & (index - step >= 0)
        valid = jnp.where(step == 0, lower, whole)
        masked = jnp.where(valid[None], scores, jnp.float32(-1e30))
        return (onehot, key_heads, masked, valid, dprob)

    def forward_step(stats, key_blk, value_blk, step):
        most, total, accum = stats
        _, _, masked, valid, dprob = pair_terms(key_blk, value_blk, step)
        top = jnp.maximum(most, masked.max(axis=-1))
        weights = jnp.where(valid[None], jnp.exp(masked - top[..., None]), jnp.float32(0.0))
        factor = jnp.exp(most - top)
        return (
            top,
            total * factor + weights.sum(axis=-1),
            accum * factor + (weights * dprob).sum(axis=-1),
        )

    zeros_rows = jnp.zeros((heads, tok), jnp.float32)
    stats = forward_step(
        (jnp.full((heads, tok), -1e30, jnp.float32), zeros_rows, zeros_rows), keys, values, 0
    )
    stash = (
        jnp.zeros((span, tok, width), keys.dtype).at[0].set(keys),
        jnp.zeros((span, tok, width), values.dtype).at[0].set(values),
    )

    def forward_loop(step, carry):
        key_blk, value_blk, stats, stash = carry
        key_blk, value_blk = passed_along((key_blk, value_blk), "seq", 1)
        stats = forward_step(stats, key_blk, value_blk, step)
        stash = (
            lax.dynamic_update_index_in_dim(stash[0], key_blk, step, 0),
            lax.dynamic_update_index_in_dim(stash[1], value_blk, step, 0),
        )
        return (key_blk, value_blk, stats, stash)

    _, _, stats, stash = lax.fori_loop(1, span, forward_loop, (keys, values, stats, stash))
    most, total, accum = stats
    lse = most + jnp.log(total)
    delta = accum / total

    def backward_terms(key_blk, value_blk, step):
        onehot, key_heads, masked, valid, dprob = pair_terms(key_blk, value_blk, step)
        prob = jnp.exp(masked - lse[..., None])
        dscore = prob * (dprob - delta[..., None])
        score16 = dscore.astype(jnp.bfloat16)
        prob16 = prob.astype(jnp.bfloat16)
        grad_q = scale * jnp.einsum(
            "hqk,khd->qhd", score16, key_heads, preferred_element_type=jnp.float32
        ).reshape(tok, width)
        grad_k = scale * jnp.einsum(
            "hqk,qhd->khd", score16, query_heads, preferred_element_type=jnp.float32
        ).reshape(tok, width)
        grad_v = jnp.einsum(
            "hqk,qhd->khd", prob16, cot_heads, preferred_element_type=jnp.float32
        ).reshape(tok, width)
        grad_b = jnp.dot(diagonal_sums(dscore), onehot, precision=highest)
        return (grad_q, grad_k, grad_v, grad_b)

    last = span - 1
    first_terms = backward_terms(stash[0][last], stash[1][last], last)

    def chain_loop(turn, carry):
        grad_q, grad_k, grad_v, grad_b = carry
        step = span - 2 - turn
        grad_k, grad_v = passed_along((grad_k, grad_v), "seq", -1)
        key_blk = lax.dynamic_index_in_dim(stash[0], step, 0, keepdims=False)
        value_blk = lax.dynamic_index_in_dim(stash[1], step, 0, keepdims=False)
        more = backward_terms(key_blk, value_blk, step)
        return (grad_q + more[0], grad_k + more[1], grad_v + more[2], grad_b + more[3])

    grad_q, grad_k, grad_v, grad_b = lax.fori_loop(0, span - 1, chain_loop, first_terms)
    key_grad = grad_k.astype(jnp.bfloat16)
    value_grad = grad_v.astype(jnp.bfloat16)
    summed = lax.psum(grad_b, "seq")
    grad_bias = lax.all_gather(summed, "head", axis=0, tiled=True)
    return (grad_q.astype(jnp.bfloat16), key_grad, value_grad, grad_bias)


def solution(mesh):
    placed = (
        P("seq", "head"),
        P("seq", "head"),
        P("seq", "head"),
        P("seq", "head"),
        P("head", None),
        P("seq", None, None),
        P("seq", None),
    )
    return jax.shard_map(
        body,
        mesh=mesh,
        in_specs=placed,
        out_specs=(P("seq", "head"), P("seq", "head"), P("seq", "head"), P()),
        check_vma=False,
    )
```

profile of v0, /device:TPU:0, one launch (start us, length us, event | category | flops | bytes accessed | tf_op | source)
XLA Modules:
  0.0 294.3 jit_solution(14736967456666874631)
XLA Ops:
  1.8 1.8 copy.44
  5.7 2.5 tile.67
  8.1 2.2 slice.162
  10.3 4.5 %reshape.290 = f32[16,128,254]{2,1,0:T(8,128)} reshape(f32[16,32512]{1,0:T(8,128)S(1)} %slice.162) | data formatting | bytes 4161536 | tf_op jit(solution)/shard_map/reshape | solution.py:27
  18.2 1.4 fusion.39
  21.1 2.0 scatter.9
  23.1 72.6 %while.52 = (s32[]{:T(128)}, bf16[128,1024]{0,1:T(8,128)(2,1)S(1)}, bf16[128,1024]{0,1:T(8,128)(2,1)}, f32[16,128]{1,0:T(8,128)S(1)}, f32[16,128]{1,0:T(8,128)S(...) while((s32[]{:T(128)}, bf16[128,1024]{0,1:T(8,128)(2,1)S(1)}, ...), condition=%wide.region_7.8_spmd.clone, body=%wide.region_3.7_spmd.clone.sunk | while | flops 76355592 | bytes 29592764 | solution.py:98
  23.1 4.9 %collective-permute-start = (bf16[128,1024]{0,1:T(8,128)(2,1)S(1)}, bf16[128,1024]{0,1:T(8,128)(2,1)S(1)}, u32[]{:S(2)}, u32[]{:S(2)}) collective-permute-start(bf16[128,1024]{0,1:T(8,128)(2,1)S(1)} %get-tuple-element.1186), channel_id=1, source_target_pairs={{0,2},{2,4},{4,6},{6,8},{8,10},{10,12},{12,14},{14,16},{16,18},{18... | collective-permute-start | bytes 786440 | tf_op jit(solution)/shard_map/while/body/eval_jaxpr/ppermute | solution.py:10
  28.0 3.4 %collective-permute-start.1 = (bf16[128,1024]{0,1:T(8,128)(2,1)}, bf16[128,1024]{0,1:T(8,128)(2,1)S(1)}, u32[]{:S(2)}, u32[]{:S(2)}) collective-permute-start(bf16[128,1024]{0,1:T(8,128)(2,1)} %get-tuple-element.1187), channel_id=1, source_target_pairs={{0,2},{2,4},{4,6},{6,8},{8,10},{10,12},{12,14},{14,16},{16,18},{18... | collective-permute-start | bytes 786440 | tf_op jit(solution)/shard_map/while/body/eval_jaxpr/ppermute | solution.py:10
  32.1 2.5 tile.79
  34.6 2.2 slice.180
  36.8 4.5 %reshape.311 = f32[16,128,254]{2,1,0:T(8,128)} reshape(f32[16,32512]{1,0:T(8,128)S(1)} %slice.180) | data formatting | bytes 4161536 | tf_op jit(solution)/shard_map/while/body/eval_jaxpr/reshape | solution.py:27
  44.8 1.4 fusion.115
  48.3 3.4 %collective-permute-start = (bf16[128,1024]{0,1:T(8,128)(2,1)S(1)}, bf16[128,1024]{0,1:T(8,128)(2,1)S(1)}, u32[]{:S(2)}, u32[]{:S(2)}) collective-permute-start(bf16[128,1024]{0,1:T(8,128)(2,1)S(1)} %get-tuple-element.1186), channel_id=1, source_target_pairs={{0,2},{2,4},{4,6},{6,8},{8,10},{10,12},{12,14},{14,16},{16,18},{18... | collective-permute-start | bytes 786440 | tf_op jit(solution)/shard_map/while/body/eval_jaxpr/ppermute | solution.py:10
  51.7 3.4 %collective-permute-start.1 = (bf16[128,1024]{0,1:T(8,128)(2,1)}, bf16[128,1024]{0,1:T(8,128)(2,1)S(1)}, u32[]{:S(2)}, u32[]{:S(2)}) collective-permute-start(bf16[128,1024]{0,1:T(8,128)(2,1)} %get-tuple-element.1187), channel_id=1, source_target_pairs={{0,2},{2,4},{4,6},{6,8},{8,10},{10,12},{12,14},{14,16},{16,18},{18... | collective-permute-start | bytes 786440 | tf_op jit(solution)/shard_map/while/body/eval_jaxpr/ppermute | solution.py:10
  55.8 2.5 tile.79
  58.3 2.2 slice.180
  60.5 4.5 %reshape.311 = f32[16,128,254]{2,1,0:T(8,128)} reshape(f32[16,32512]{1,0:T(8,128)S(1)} %slice.180) | data formatting | bytes 4161536 | tf_op jit(solution)/shard_map/while/body/eval_jaxpr/reshape | solution.py:27
  68.5 1.4 fusion.115
  72.0 3.4 %collective-permute-start = (bf16[128,1024]{0,1:T(8,128)(2,1)S(1)}, bf16[128,1024]{0,1:T(8,128)(2,1)S(1)}, u32[]{:S(2)}, u32[]{:S(2)}) collective-permute-start(bf16[128,1024]{0,1:T(8,128)(2,1)S(1)} %get-tuple-element.1186), channel_id=1, source_target_pairs={{0,2},{2,4},{4,6},{6,8},{8,10},{10,12},{12,14},{14,16},{16,18},{18... | collective-permute-start | bytes 786440 | tf_op jit(solution)/shard_map/while/body/eval_jaxpr/ppermute | solution.py:10
  75.4 3.4 %collective-permute-start.1 = (bf16[128,1024]{0,1:T(8,128)(2,1)}, bf16[128,1024]{0,1:T(8,128)(2,1)S(1)}, u32[]{:S(2)}, u32[]{:S(2)}) collective-permute-start(bf16[128,1024]{0,1:T(8,128)(2,1)} %get-tuple-element.1187), channel_id=1, source_target_pairs={{0,2},{2,4},{4,6},{6,8},{8,10},{10,12},{12,14},{14,16},{16,18},{18... | collective-permute-start | bytes 786440 | tf_op jit(solution)/shard_map/while/body/eval_jaxpr/ppermute | solution.py:10
  79.5 2.5 tile.79
  82.0 2.2 slice.180
  84.2 4.5 %reshape.311 = f32[16,128,254]{2,1,0:T(8,128)} reshape(f32[16,32512]{1,0:T(8,128)S(1)} %slice.180) | data formatting | bytes 4161536 | tf_op jit(solution)/shard_map/while/body/eval_jaxpr/reshape | solution.py:27
  92.1 1.4 fusion.115
  95.7 1.7 slice.141
  98.1 2.5 tile.69
  100.6 2.2 slice.165
  102.8 4.5 %reshape.295 = f32[16,128,254]{2,1,0:T(8,128)} reshape(f32[16,32512]{1,0:T(8,128)S(1)} %slice.165) | data formatting | bytes 4161536 | tf_op jit(solution)/shard_map/reshape | solution.py:27
  110.2 1.4 fusion.36
  116.3 2.2 fusion.41
  120.6 1.5 slice.167
  122.1 4.8 %reshape.298 = f32[16,128,255]{2,1,0:T(8,128)S(1)} reshape(f32[16,32640]{1,0:T(8,128)} %slice.167) | data formatting | bytes 4177920 | tf_op jit(solution)/shard_map/reshape | solution.py:18
  127.3 105.1 %while.53 = (s32[]{:T(128)}, f32[128,1024]{0,1:T(8,128)}, f32[128,1024]{0,1:T(8,128)}, f32[128,1024]{0,1:T(8,128)}, f32[16,128]{1,0:T(8,128)S(1)}, /*index=5*/bf...) while((s32[]{:T(128)}, f32[128,1024]{0,1:T(8,128)}, ...), condition=%wide.region_11.12_spmd.clone, body=%wide.region_9.11_spmd.clone.sunk | while | flops 183988240 | bytes 71119040 | solution.py:133
  130.8 2.5 tile.81
  133.2 2.2 slice.183
  135.4 4.5 %reshape.312 = f32[16,128,254]{2,1,0:T(8,128)} reshape(f32[16,32512]{1,0:T(8,128)S(1)} %slice.183) | data formatting | bytes 4161536 | tf_op jit(solution)/shard_map/while/body/eval_jaxpr/reshape | solution.py:27
  150.1 1.5 slice.185
  151.6 4.8 %reshape.313 = f32[16,128,255]{2,1,0:T(8,128)S(1)} reshape(f32[16,32640]{1,0:T(8,128)} %slice.185) | data formatting | bytes 4177920 | tf_op jit(solution)/shard_map/while/body/eval_jaxpr/reshape | solution.py:18
  156.8 1.5 fusion.132
  158.5 2.1 bitcast_add_fusion.7
  160.6 1.9 bitcast_add_fusion.8
  165.7 2.5 tile.81
  168.2 2.2 slice.183
  170.4 4.5 %reshape.312 = f32[16,128,254]{2,1,0:T(8,128)} reshape(f32[16,32512]{1,0:T(8,128)S(1)} %slice.183) | data formatting | bytes 4161536 | tf_op jit(solution)/shard_map/while/body/eval_jaxpr/reshape | solution.py:27
  185.1 1.5 slice.185
  186.5 4.8 %reshape.313 = f32[16,128,255]{2,1,0:T(8,128)S(1)} reshape(f32[16,32640]{1,0:T(8,128)} %slice.185) | data formatting | bytes 4177920 | tf_op jit(solution)/shard_map/while/body/eval_jaxpr/reshape | solution.py:18
  191.8 1.5 fusion.132
  193.5 2.1 bitcast_add_fusion.7
  195.5 1.9 bitcast_add_fusion.8
  200.7 2.5 tile.81
  203.2 2.2 slice.183
  205.4 4.5 %reshape.312 = f32[16,128,254]{2,1,0:T(8,128)} reshape(f32[16,32512]{1,0:T(8,128)S(1)} %slice.183) | data formatting | bytes 4161536 | tf_op jit(solution)/shard_map/while/body/eval_jaxpr/reshape | solution.py:27
  214.2 1.3 fusion.131
  220.0 1.5 slice.185
  221.5 4.8 %reshape.313 = f32[16,128,255]{2,1,0:T(8,128)S(1)} reshape(f32[16,32640]{1,0:T(8,128)} %slice.185) | data formatting | bytes 4177920 | tf_op jit(solution)/shard_map/while/body/eval_jaxpr/reshape | solution.py:18
  226.8 1.5 fusion.132
  228.4 2.1 bitcast_add_fusion.7
  230.5 1.9 bitcast_add_fusion.8
  232.4 1.9 copy.50
  234.3 1.9 copy.51
  236.2 1.9 copy.52
  238.0 53.8 %psum.7 = f32[16,128]{1,0:T(8,128)S(1)} all-reduce(f32[16,128]{1,0:T(8,128)S(1)} %get-tuple-element.814), channel_id=1, replica_groups=mesh['seq'=16,'head'=2] {'seq'}, use_global_device_ids=true, to_apply=%region_12.13 | all-reduce | flops 2048 | bytes 16384 | tf_op jit(solution)/shard_map/psum | solution.py:136
  291.9 1.8 all_gather.3
  (213 shorter events, 73.4 us)
Async XLA Ops:
  14.9 1.2 slice-start.2
  14.9 1.6 copy-start.5
  16.4 1.0 copy-start.6
  19.7 3.4 %copy-start.7 = (s32[1,4,256]{2,1,0:T(4,128)S(1)}, s32[1,4,256]{2,1,0:T(4,128)}, u32[]{:S(2)}) copy-start(s32[1,4,256]{2,1,0:T(4,128)} %param.20) | copy-start | bytes 12292
  19.7 3.4 %copy-start.8 = (f32[16,128]{1,0:T(8,128)S(1)}, f32[16,128]{1,0:T(8,128)}, u32[]{:S(2)}) copy-start(f32[16,128]{1,0:T(8,128)} %param.19) | copy-start | bytes 24580
  19.7 3.4 %copy-start.9 = (s32[1,4]{1,0:T(1,128)S(1)}, s32[1,4]{1,0:T(1,128)}, u32[]{:S(2)}) copy-start(s32[1,4]{1,0:T(1,128)} %param.21) | copy-start | bytes 52
  23.1 21.0 %collective-permute-start = (bf16[128,1024]{0,1:T(8,128)(2,1)S(1)}, bf16[128,1024]{0,1:T(8,128)(2,1)S(1)}, u32[]{:S(2)}, u32[]{:S(2)}) collective-permute-start(bf16[128,1024]{0,1:T(8,128)(2,1)S(1)} %get-tuple-element.1186), channel_id=1, source_target_pairs={{0,2},{2,4},{4,6},{6,8},{8,10},{10,12},{12,14},{14,16},{16,18},{18... | collective-permute-start | bytes 786440 | tf_op jit(solution)/shard_map/while/body/eval_jaxpr/ppermute | solution.py:10
  28.0 16.7 %collective-permute-start.1 = (bf16[128,1024]{0,1:T(8,128)(2,1)}, bf16[128,1024]{0,1:T(8,128)(2,1)S(1)}, u32[]{:S(2)}, u32[]{:S(2)}) collective-permute-start(bf16[128,1024]{0,1:T(8,128)(2,1)} %get-tuple-element.1187), channel_id=1, source_target_pairs={{0,2},{2,4},{4,6},{6,8},{8,10},{10,12},{12,14},{14,16},{16,18},{18... | collective-permute-start | bytes 786440 | tf_op jit(solution)/shard_map/while/body/eval_jaxpr/ppermute | solution.py:10
  41.3 1.2 slice-start
  48.3 19.5 %collective-permute-start = (bf16[128,1024]{0,1:T(8,128)(2,1)S(1)}, bf16[128,1024]{0,1:T(8,128)(2,1)S(1)}, u32[]{:S(2)}, u32[]{:S(2)}) collective-permute-start(bf16[128,1024]{0,1:T(8,128)(2,1)S(1)} %get-tuple-element.1186), channel_id=1, source_target_pairs={{0,2},{2,4},{4,6},{6,8},{8,10},{10,12},{12,14},{14,16},{16,18},{18... | collective-permute-start | bytes 786440 | tf_op jit(solution)/shard_map/while/body/eval_jaxpr/ppermute | solution.py:10
  51.7 16.7 %collective-permute-start.1 = (bf16[128,1024]{0,1:T(8,128)(2,1)}, bf16[128,1024]{0,1:T(8,128)(2,1)S(1)}, u32[]{:S(2)}, u32[]{:S(2)}) collective-permute-start(bf16[128,1024]{0,1:T(8,128)(2,1)} %get-tuple-element.1187), channel_id=1, source_target_pairs={{0,2},{2,4},{4,6},{6,8},{8,10},{10,12},{12,14},{14,16},{16,18},{18... | collective-permute-start | bytes 786440 | tf_op jit(solution)/shard_map/while/body/eval_jaxpr/ppermute | solution.py:10
  65.0 1.2 slice-start
  72.0 19.5 %collective-permute-start = (bf16[128,1024]{0,1:T(8,128)(2,1)S(1)}, bf16[128,1024]{0,1:T(8,128)(2,1)S(1)}, u32[]{:S(2)}, u32[]{:S(2)}) collective-permute-start(bf16[128,1024]{0,1:T(8,128)(2,1)S(1)} %get-tuple-element.1186), channel_id=1, source_target_pairs={{0,2},{2,4},{4,6},{6,8},{8,10},{10,12},{12,14},{14,16},{16,18},{18... | collective-permute-start | bytes 786440 | tf_op jit(solution)/shard_map/while/body/eval_jaxpr/ppermute | solution.py:10
  75.4 16.7 %collective-permute-start.1 = (bf16[128,1024]{0,1:T(8,128)(2,1)}, bf16[128,1024]{0,1:T(8,128)(2,1)S(1)}, u32[]{:S(2)}, u32[]{:S(2)}) collective-permute-start(bf16[128,1024]{0,1:T(8,128)(2,1)} %get-tuple-element.1187), channel_id=1, source_target_pairs={{0,2},{2,4},{4,6},{6,8},{8,10},{10,12},{12,14},{14,16},{16,18},{18... | collective-permute-start | bytes 786440 | tf_op jit(solution)/shard_map/while/body/eval_jaxpr/ppermute | solution.py:10
  88.7 1.2 slice-start
  107.3 1.2 slice-start.3
  111.6 2.3 copy-start.4
  127.5 31.0 %collective-permute-start.2 = (f32[128,1024]{0,1:T(8,128)}, f32[128,1024]{0,1:T(8,128)}, u32[]{:S(2)}, u32[]{:S(2)}) collective-permute-start(f32[128,1024]{0,1:T(8,128)} %get-tuple-element.1244), channel_id=1, source_target_pairs={{2,0},{4,2},{6,4},{8,6},{10,8},{12,10},{14,12},{16,14},{18,16},{20... | collective-permute-start | bytes 1572872 | tf_op jit(solution)/shard_map/while/body/eval_jaxpr/ppermute | solution.py:10
  128.8 31.8 %collective-permute-start.3 = (f32[128,1024]{0,1:T(8,128)}, f32[128,1024]{0,1:T(8,128)}, u32[]{:S(2)}, u32[]{:S(2)}) collective-permute-start(f32[128,1024]{0,1:T(8,128)} %get-tuple-element.1245), channel_id=1, source_target_pairs={{2,0},{4,2},{6,4},{8,6},{10,8},{12,10},{14,12},{16,14},{18,16},{20... | collective-permute-start | bytes 1572872 | tf_op jit(solution)/shard_map/while/body/eval_jaxpr/ppermute | solution.py:10
  140.0 1.2 slice-start.1
  156.6 1.8 copy-start.1
  156.6 1.8 copy-start.2
  156.6 1.9 copy-start
  158.5 4.0 %copy-start.3 = (f32[128,1024]{0,1:T(8,128)}, f32[128,1024]{0,1:T(8,128)S(1)}, u32[]{:S(2)}) copy-start(f32[128,1024]{0,1:T(8,128)S(1)} %bitcast_add_fusion.6) | copy-start | bytes 1572868 | tf_op jit(solution)/shard_map/while
  162.5 31.0 %collective-permute-start.2 = (f32[128,1024]{0,1:T(8,128)}, f32[128,1024]{0,1:T(8,128)}, u32[]{:S(2)}, u32[]{:S(2)}) collective-permute-start(f32[128,1024]{0,1:T(8,128)} %get-tuple-element.1244), channel_id=1, source_target_pairs={{2,0},{4,2},{6,4},{8,6},{10,8},{12,10},{14,12},{16,14},{18,16},{20... | collective-permute-start | bytes 1572872 | tf_op jit(solution)/shard_map/while/body/eval_jaxpr/ppermute | solution.py:10
  163.7 31.8 %collective-permute-start.3 = (f32[128,1024]{0,1:T(8,128)}, f32[128,1024]{0,1:T(8,128)}, u32[]{:S(2)}, u32[]{:S(2)}) collective-permute-start(f32[128,1024]{0,1:T(8,128)} %get-tuple-element.1245), channel_id=1, source_target_pairs={{2,0},{4,2},{6,4},{8,6},{10,8},{12,10},{14,12},{16,14},{18,16},{20... | collective-permute-start | bytes 1572872 | tf_op jit(solution)/shard_map/while/body/eval_jaxpr/ppermute | solution.py:10
  174.9 1.2 slice-start.1
  191.5 1.8 copy-start.1
  191.5 1.8 copy-start.2
  191.5 1.9 copy-start
  193.4 4.0 %copy-start.3 = (f32[128,1024]{0,1:T(8,128)}, f32[128,1024]{0,1:T(8,128)S(1)}, u32[]{:S(2)}) copy-start(f32[128,1024]{0,1:T(8,128)S(1)} %bitcast_add_fusion.6) | copy-start | bytes 1572868 | tf_op jit(solution)/shard_map/while
  197.4 31.0 %collective-permute-start.2 = (f32[128,1024]{0,1:T(8,128)}, f32[128,1024]{0,1:T(8,128)}, u32[]{:S(2)}, u32[]{:S(2)}) collective-permute-start(f32[128,1024]{0,1:T(8,128)} %get-tuple-element.1244), channel_id=1, source_target_pairs={{2,0},{4,2},{6,4},{8,6},{10,8},{12,10},{14,12},{16,14},{18,16},{20... | collective-permute-start | bytes 1572872 | tf_op jit(solution)/shard_map/while/body/eval_jaxpr/ppermute | solution.py:10
  198.7 31.8 %collective-permute-start.3 = (f32[128,1024]{0,1:T(8,128)}, f32[128,1024]{0,1:T(8,128)}, u32[]{:S(2)}, u32[]{:S(2)}) collective-permute-start(f32[128,1024]{0,1:T(8,128)} %get-tuple-element.1245), channel_id=1, source_target_pairs={{2,0},{4,2},{6,4},{8,6},{10,8},{12,10},{14,12},{16,14},{18,16},{20... | collective-permute-start | bytes 1572872 | tf_op jit(solution)/shard_map/while/body/eval_jaxpr/ppermute | solution.py:10
  209.9 1.2 slice-start.1
  226.5 1.8 copy-start.1
  226.5 1.8 copy-start.2
  226.5 1.9 copy-start
  228.4 4.0 %copy-start.3 = (f32[128,1024]{0,1:T(8,128)}, f32[128,1024]{0,1:T(8,128)S(1)}, u32[]{:S(2)}) copy-start(f32[128,1024]{0,1:T(8,128)S(1)} %bitcast_add_fusion.6) | copy-start | bytes 1572868 | tf_op jit(solution)/shard_map/while
where the time goes:
time: 297 us; the launch traced here: 294 us
  local copies, waits for them, and re-layouts  154 us (52%)
  blocking collectives  55.6 us (19%)
  matrix products  34.3 us (12%)
  starting transfers between devices  29.6 us (10%)
  other arithmetic  13.8 us (5%)
  loops' own time  5.03 us (2%)
    psum x1, blocking collectives, body(): summed = lax.psum(grad_b, 'seq')  53.8 us
    reshape x8, local copies, waits for them, and re-layouts, toeplitz_rows(): return window.reshape(heads, rows, 2 * rows - 2)[:, :, :rows]  36.3 us
    ppermute x12, starting transfers between devices, passed_along(): return lax.ppermute(value, axis, pairs)  29.6 us
    another operation x16, local copies, waits for them, and re-layouts, toeplitz_rows(): tiled = jnp.tile(reverse, (1, rows))  21.1 us
    reshape x4, local copies, waits for them, and re-layouts, diagonal_sums(): sums = sheared.reshape(heads, rows, 2 * rows - 1).sum(axis=1)  19.2 us
    slice x8, local copies, waits for them, and re-layouts, toeplitz_rows(): window = tiled[:, rows - 1:rows - 1 + rows * (2 * rows - 2)]  17.5 us
    dot_general x8, matrix products, pair_terms(): jnp.einsum('qhd,khd->hqk', cot_heads, value_heads, preferred_element_type...  10.8 us
    while x57, local copies, waits for them, and re-layouts  10.6 us
  transfers between devices with their start and end apart: 12, of which 0 were waited for; matrix products, arithmetic and copies ran while one was open for 41% of the time, Pallas kernels for 0%

commit v1 on v0

--- a/solution.py
+++ b/solution.py
@@ -133,7 +133,9 @@
     grad_q, grad_k, grad_v, grad_b = lax.fori_loop(0, span - 1, chain_loop, first_terms)
     key_grad = grad_k.astype(jnp.bfloat16)
     value_grad = grad_v.astype(jnp.bfloat16)
-    summed = lax.psum(grad_b, "seq")
+    summed = grad_b
+    for hop in (1, 2, 4, 8):
+        summed = summed + lax.ppermute(summed, "seq", [(dev, dev ^ hop) for dev in range(16)])
     grad_bias = lax.all_gather(summed, "head", axis=0, tiled=True)
     return (grad_q.astype(jnp.bfloat16), key_grad, value_grad, grad_bias)
 

time: 297 us -> 269 us (0.906)
  blocking collectives: 55.6 us -> 1.81 us
  starting transfers between devices: 29.6 us -> 49.6 us
  waiting for transfers between devices: 0.03 us -> 4.92 us
    psum x1 -> x0, blocking collectives: 53.8 us -> none  [body(): summed = lax.psum(grad_b, 'seq')]
    ppermute x0 -> x4, starting transfers between devices: none -> 20.1 us  [body(): lax.ppermute(summed, 'seq', [(dev, dev ^ hop) for dev in range(16)])]
    ppermute x0 -> x4, waiting for transfers between devices: none -> 4.89 us  [body(): lax.ppermute(summed, 'seq', [(dev, dev ^ hop) for dev in range(16)])]
    unnamed x25 -> x27, local copies, waits for them, and re-layouts: 7.77 us -> 7.78 us
  transfers between devices with their start and end apart: 12 -> 16, of which waited for: 0 -> 3; matrix products, arithmetic and copies ran while one was open for 41% -> 47% of each run, Pallas kernels for 0% -> 0%
where the time goes in v1:
time: 269 us; the launch traced here: 266 us
  local copies, waits for them, and re-layouts  155 us (58%)
  starting transfers between devices  49.6 us (18%)
  matrix products  34.4 us (13%)
  other arithmetic  13.7 us (5%)
  loops' own time  5.07 us (2%)
  waiting for transfers between devices  4.92 us (2%)
    reshape x8, local copies, waits for them, and re-layouts, toeplitz_rows(): return window.reshape(heads, rows, 2 * rows - 2)[:, :, :rows]  36.4 us
    ppermute x12, starting transfers between devices, passed_along(): return lax.ppermute(value, axis, pairs)  29.6 us
    another operation x16, local copies, waits for them, and re-layouts, toeplitz_rows(): tiled = jnp.tile(reverse, (1, rows))  21.1 us
    ppermute x4, starting transfers between devices, body(): lax.ppermute(summed, 'seq', [(dev, dev ^ hop) for dev in range(16)])  20.1 us
    reshape x4, local copies, waits for them, and re-layouts, diagonal_sums(): sums = sheared.reshape(heads, rows, 2 * rows - 1).sum(axis=1)  19.2 us
    slice x8, local copies, waits for them, and re-layouts, toeplitz_rows(): window = tiled[:, rows - 1:rows - 1 + rows * (2 * rows - 2)]  17.5 us
    dot_general x8, matrix products, pair_terms(): jnp.einsum('qhd,khd->hqk', cot_heads, value_heads, preferred_element_type...  10.8 us
    while x57, local copies, waits for them, and re-layouts  10.6 us
  transfers between devices with their start and end apart: 16, of which 3 were waited for; matrix products, arithmetic and copies ran while one was open for 47% of the time, Pallas kernels for 0%

profile of v1, /device:TPU:0, one launch (start us, length us, event | category | flops | bytes accessed | tf_op | source)
XLA Modules:
  0.0 266.4 jit_solution(17154243849417206901)
XLA Ops:
  1.8 1.8 copy.44
  5.7 2.5 tile.67
  8.2 2.2 slice.162
  10.3 4.5 %reshape.290 = f32[16,128,254]{2,1,0:T(8,128)} reshape(f32[16,32512]{1,0:T(8,128)S(1)} %slice.162) | data formatting | bytes 4161536 | tf_op jit(solution)/shard_map/reshape | solution.py:27
  19.4 2.1 scatter.9
  23.8 72.8 %while.52 = (s32[]{:T(128)}, bf16[128,1024]{0,1:T(8,128)(2,1)S(1)}, bf16[128,1024]{0,1:T(8,128)(2,1)}, f32[16,128]{1,0:T(8,128)S(1)}, f32[16,128]{1,0:T(8,128)S(...) while((s32[]{:T(128)}, bf16[128,1024]{0,1:T(8,128)(2,1)S(1)}, ...), condition=%wide.region_7.8_spmd.clone, body=%wide.region_3.7_spmd.clone.sunk | while | flops 76355592 | bytes 29592764 | solution.py:98
  23.8 4.9 %collective-permute-start = (bf16[128,1024]{0,1:T(8,128)(2,1)S(1)}, bf16[128,1024]{0,1:T(8,128)(2,1)S(1)}, u32[]{:S(2)}, u32[]{:S(2)}) collective-permute-start(bf16[128,1024]{0,1:T(8,128)(2,1)S(1)} %get-tuple-element.1186), channel_id=1, source_target_pairs={{0,2},{2,4},{4,6},{6,8},{8,10},{10,12},{12,14},{14,16},{16,18},{18... | collective-permute-start | bytes 786440 | tf_op jit(solution)/shard_map/while/body/eval_jaxpr/ppermute | solution.py:10
  28.7 3.4 %collective-permute-start.1 = (bf16[128,1024]{0,1:T(8,128)(2,1)}, bf16[128,1024]{0,1:T(8,128)(2,1)S(1)}, u32[]{:S(2)}, u32[]{:S(2)}) collective-permute-start(bf16[128,1024]{0,1:T(8,128)(2,1)} %get-tuple-element.1187), channel_id=1, source_target_pairs={{0,2},{2,4},{4,6},{6,8},{8,10},{10,12},{12,14},{14,16},{16,18},{18... | collective-permute-start | bytes 786440 | tf_op jit(solution)/shard_map/while/body/eval_jaxpr/ppermute | solution.py:10
  32.8 2.5 tile.79
  35.3 2.2 slice.180
  37.5 4.5 %reshape.311 = f32[16,128,254]{2,1,0:T(8,128)} reshape(f32[16,32512]{1,0:T(8,128)S(1)} %slice.180) | data formatting | bytes 4161536 | tf_op jit(solution)/shard_map/while/body/eval_jaxpr/reshape | solution.py:27
  49.1 3.4 %collective-permute-start = (bf16[128,1024]{0,1:T(8,128)(2,1)S(1)}, bf16[128,1024]{0,1:T(8,128)(2,1)S(1)}, u32[]{:S(2)}, u32[]{:S(2)}) collective-permute-start(bf16[128,1024]{0,1:T(8,128)(2,1)S(1)} %get-tuple-element.1186), channel_id=1, source_target_pairs={{0,2},{2,4},{4,6},{6,8},{8,10},{10,12},{12,14},{14,16},{16,18},{18... | collective-permute-start | bytes 786440 | tf_op jit(solution)/shard_map/while/body/eval_jaxpr/ppermute | solution.py:10
  52.5 3.4 %collective-permute-start.1 = (bf16[128,1024]{0,1:T(8,128)(2,1)}, bf16[128,1024]{0,1:T(8,128)(2,1)S(1)}, u32[]{:S(2)}, u32[]{:S(2)}) collective-permute-start(bf16[128,1024]{0,1:T(8,128)(2,1)} %get-tuple-element.1187), channel_id=1, source_target_pairs={{0,2},{2,4},{4,6},{6,8},{8,10},{10,12},{12,14},{14,16},{16,18},{18... | collective-permute-start | bytes 786440 | tf_op jit(solution)/shard_map/while/body/eval_jaxpr/ppermute | solution.py:10
  56.5 2.5 tile.79
  59.0 2.2 slice.180
  61.2 4.5 %reshape.311 = f32[16,128,254]{2,1,0:T(8,128)} reshape(f32[16,32512]{1,0:T(8,128)S(1)} %slice.180) | data formatting | bytes 4161536 | tf_op jit(solution)/shard_map/while/body/eval_jaxpr/reshape | solution.py:27
  72.8 3.4 %collective-permute-start = (bf16[128,1024]{0,1:T(8,128)(2,1)S(1)}, bf16[128,1024]{0,1:T(8,128)(2,1)S(1)}, u32[]{:S(2)}, u32[]{:S(2)}) collective-permute-start(bf16[128,1024]{0,1:T(8,128)(2,1)S(1)} %get-tuple-element.1186), channel_id=1, source_target_pairs={{0,2},{2,4},{4,6},{6,8},{8,10},{10,12},{12,14},{14,16},{16,18},{18... | collective-permute-start | bytes 786440 | tf_op jit(solution)/shard_map/while/body/eval_jaxpr/ppermute | solution.py:10
  76.2 3.4 %collective-permute-start.1 = (bf16[128,1024]{0,1:T(8,128)(2,1)}, bf16[128,1024]{0,1:T(8,128)(2,1)S(1)}, u32[]{:S(2)}, u32[]{:S(2)}) collective-permute-start(bf16[128,1024]{0,1:T(8,128)(2,1)} %get-tuple-element.1187), channel_id=1, source_target_pairs={{0,2},{2,4},{4,6},{6,8},{8,10},{10,12},{12,14},{14,16},{16,18},{18... | collective-permute-start | bytes 786440 | tf_op jit(solution)/shard_map/while/body/eval_jaxpr/ppermute | solution.py:10
  80.3 2.5 tile.79
  82.8 2.2 slice.180
  85.0 4.5 %reshape.311 = f32[16,128,254]{2,1,0:T(8,128)} reshape(f32[16,32512]{1,0:T(8,128)S(1)} %slice.180) | data formatting | bytes 4161536 | tf_op jit(solution)/shard_map/while/body/eval_jaxpr/reshape | solution.py:27
  96.6 1.7 slice.141
  99.0 2.5 tile.69
  101.4 2.2 slice.165
  103.6 4.5 %reshape.295 = f32[16,128,254]{2,1,0:T(8,128)} reshape(f32[16,32512]{1,0:T(8,128)S(1)} %slice.165) | data formatting | bytes 4161536 | tf_op jit(solution)/shard_map/reshape | solution.py:27
  109.7 1.7 slice.145
  117.3 2.2 fusion.41
  121.7 1.5 slice.167
  123.2 4.8 %reshape.298 = f32[16,128,255]{2,1,0:T(8,128)S(1)} reshape(f32[16,32640]{1,0:T(8,128)} %slice.167) | data formatting | bytes 4177920 | tf_op jit(solution)/shard_map/reshape | solution.py:18
  128.4 105.0 %while.53 = (s32[]{:T(128)}, f32[128,1024]{0,1:T(8,128)}, f32[128,1024]{0,1:T(8,128)}, f32[128,1024]{0,1:T(8,128)}, f32[16,128]{1,0:T(8,128)S(1)}, /*index=5*/bf...) while((s32[]{:T(128)}, f32[128,1024]{0,1:T(8,128)}, ...), condition=%wide.region_11.12_spmd.clone, body=%wide.region_9.11_spmd.clone.sunk | while | flops 183988240 | bytes 71119040 | solution.py:133
  131.8 2.5 tile.81
  134.3 2.2 slice.183
  136.5 4.5 %reshape.312 = f32[16,128,254]{2,1,0:T(8,128)} reshape(f32[16,32512]{1,0:T(8,128)S(1)} %slice.183) | data formatting | bytes 4161536 | tf_op jit(solution)/shard_map/while/body/eval_jaxpr/reshape | solution.py:27
  151.2 1.5 slice.185
  152.6 4.8 %reshape.313 = f32[16,128,255]{2,1,0:T(8,128)S(1)} reshape(f32[16,32640]{1,0:T(8,128)} %slice.185) | data formatting | bytes 4177920 | tf_op jit(solution)/shard_map/while/body/eval_jaxpr/reshape | solution.py:18
  157.9 1.5 fusion.132
  159.5 2.1 bitcast_add_fusion.7
  161.6 1.9 bitcast_add_fusion.8
  166.8 2.5 tile.81
  169.2 2.2 slice.183
  171.4 4.5 %reshape.312 = f32[16,128,254]{2,1,0:T(8,128)} reshape(f32[16,32512]{1,0:T(8,128)S(1)} %slice.183) | data formatting | bytes 4161536 | tf_op jit(solution)/shard_map/while/body/eval_jaxpr/reshape | solution.py:27
  186.1 1.5 slice.185
  187.6 4.8 %reshape.313 = f32[16,128,255]{2,1,0:T(8,128)S(1)} reshape(f32[16,32640]{1,0:T(8,128)} %slice.185) | data formatting | bytes 4177920 | tf_op jit(solution)/shard_map/while/body/eval_jaxpr/reshape | solution.py:18
  192.8 1.5 fusion.132
  194.5 2.1 bitcast_add_fusion.7
  196.6 1.9 bitcast_add_fusion.8
  201.7 2.5 tile.81
  204.2 2.2 slice.183
  206.4 4.5 %reshape.312 = f32[16,128,254]{2,1,0:T(8,128)} reshape(f32[16,32512]{1,0:T(8,128)S(1)} %slice.183) | data formatting | bytes 4161536 | tf_op jit(solution)/shard_map/while/body/eval_jaxpr/reshape | solution.py:27
  222.5 4.8 %reshape.313 = f32[16,128,255]{2,1,0:T(8,128)S(1)} reshape(f32[16,32640]{1,0:T(8,128)} %slice.185) | data formatting | bytes 4177920 | tf_op jit(solution)/shard_map/while/body/eval_jaxpr/reshape | solution.py:18
  227.8 1.5 fusion.132
  229.5 2.1 bitcast_add_fusion.7
  231.5 1.9 bitcast_add_fusion.8
  233.4 5.8 %collective-permute-start.4 = (f32[16,128]{1,0:T(8,128)S(1)}, f32[16,128]{1,0:T(8,128)S(1)}, u32[]{:S(2)}, u32[]{:S(2)}) collective-permute-start(f32[16,128]{1,0:T(8,128)S(1)} %get-tuple-element.814), channel_id=1, source_target_pairs={{0,2},{2,0},{4,6},{6,4},{8,10},{10,8},{12,14},{14,12},{16,18},{18,... | collective-permute-start | bytes 24584 | tf_op jit(solution)/shard_map/ppermute | solution.py:138
  239.2 1.6 collective-permute-done.4
  240.8 3.5 %collective-permute-start.5 = (f32[16,128]{1,0:T(8,128)S(1)}, f32[16,128]{1,0:T(8,128)S(1)}, u32[]{:S(2)}, u32[]{:S(2)}) collective-permute-start(f32[16,128]{1,0:T(8,128)S(1)} %add.208), channel_id=1, source_target_pairs={{0,4},{2,6},{4,0},{6,2},{8,12},{10,14},{12,8},{14,10},{16,20},{18,... | collective-permute-start | bytes 24584 | tf_op jit(solution)/shard_map/ppermute | solution.py:138
  244.3 1.6 collective-permute-done.5
  245.9 6.4 %collective-permute-start.6 = (f32[16,128]{1,0:T(8,128)S(1)}, f32[16,128]{1,0:T(8,128)S(1)}, u32[]{:S(2)}, u32[]{:S(2)}) collective-permute-start(f32[16,128]{1,0:T(8,128)S(1)} %add.209), channel_id=1, source_target_pairs={{0,8},{2,10},{4,12},{6,14},{8,0},{10,2},{12,4},{14,6},{16,24},{18,... | collective-permute-start | bytes 24584 | tf_op jit(solution)/shard_map/ppermute | solution.py:138
  252.3 1.6 collective-permute-done.6
  253.9 4.4 %collective-permute-start.7 = (f32[16,128]{1,0:T(8,128)S(1)}, f32[16,128]{1,0:T(8,128)S(1)}, u32[]{:S(2)}, u32[]{:S(2)}) collective-permute-start(f32[16,128]{1,0:T(8,128)S(1)} %add.210), channel_id=1, source_target_pairs={{0,16},{2,18},{4,20},{6,22},{8,24},{10,26},{12,28},{14,30},{16,0},... | collective-permute-start | bytes 24584 | tf_op jit(solution)/shard_map/ppermute | solution.py:138
  258.4 1.9 copy.50
  260.3 1.9 copy.51
  262.1 1.9 copy.52
  264.0 1.8 all_gather.3
  (226 shorter events, 82.4 us)
Async XLA Ops:
  14.9 1.2 slice-start.2
  14.9 1.6 copy-start.6
  16.5 1.0 copy-start.7
  17.0 4.4 %copy-start.10 = (s32[1,4]{1,0:T(1,128)S(1)}, s32[1,4]{1,0:T(1,128)}, u32[]{:S(2)}) copy-start(s32[1,4]{1,0:T(1,128)} %param.21) | copy-start | bytes 52
  19.4 4.4 %copy-start.8 = (s32[1,4,256]{2,1,0:T(4,128)S(1)}, s32[1,4,256]{2,1,0:T(4,128)}, u32[]{:S(2)}) copy-start(s32[1,4,256]{2,1,0:T(4,128)} %param.20) | copy-start | bytes 12292
  19.4 4.4 %copy-start.9 = (f32[16,128]{1,0:T(8,128)S(1)}, f32[16,128]{1,0:T(8,128)}, u32[]{:S(2)}) copy-start(f32[16,128]{1,0:T(8,128)} %param.19) | copy-start | bytes 24580
  23.8 21.0 %collective-permute-start = (bf16[128,1024]{0,1:T(8,128)(2,1)S(1)}, bf16[128,1024]{0,1:T(8,128)(2,1)S(1)}, u32[]{:S(2)}, u32[]{:S(2)}) collective-permute-start(bf16[128,1024]{0,1:T(8,128)(2,1)S(1)} %get-tuple-element.1186), channel_id=1, source_target_pairs={{0,2},{2,4},{4,6},{6,8},{8,10},{10,12},{12,14},{14,16},{16,18},{18... | collective-permute-start | bytes 786440 | tf_op jit(solution)/shard_map/while/body/eval_jaxpr/ppermute | solution.py:10
  28.7 16.8 %collective-permute-start.1 = (bf16[128,1024]{0,1:T(8,128)(2,1)}, bf16[128,1024]{0,1:T(8,128)(2,1)S(1)}, u32[]{:S(2)}, u32[]{:S(2)}) collective-permute-start(bf16[128,1024]{0,1:T(8,128)(2,1)} %get-tuple-element.1187), channel_id=1, source_target_pairs={{0,2},{2,4},{4,6},{6,8},{8,10},{10,12},{12,14},{14,16},{16,18},{18... | collective-permute-start | bytes 786440 | tf_op jit(solution)/shard_map/while/body/eval_jaxpr/ppermute | solution.py:10
  42.0 1.2 slice-start
  49.1 19.5 %collective-permute-start = (bf16[128,1024]{0,1:T(8,128)(2,1)S(1)}, bf16[128,1024]{0,1:T(8,128)(2,1)S(1)}, u32[]{:S(2)}, u32[]{:S(2)}) collective-permute-start(bf16[128,1024]{0,1:T(8,128)(2,1)S(1)} %get-tuple-element.1186), channel_id=1, source_target_pairs={{0,2},{2,4},{4,6},{6,8},{8,10},{10,12},{12,14},{14,16},{16,18},{18... | collective-permute-start | bytes 786440 | tf_op jit(solution)/shard_map/while/body/eval_jaxpr/ppermute | solution.py:10
  52.5 16.7 %collective-permute-start.1 = (bf16[128,1024]{0,1:T(8,128)(2,1)}, bf16[128,1024]{0,1:T(8,128)(2,1)S(1)}, u32[]{:S(2)}, u32[]{:S(2)}) collective-permute-start(bf16[128,1024]{0,1:T(8,128)(2,1)} %get-tuple-element.1187), channel_id=1, source_target_pairs={{0,2},{2,4},{4,6},{6,8},{8,10},{10,12},{12,14},{14,16},{16,18},{18... | collective-permute-start | bytes 786440 | tf_op jit(solution)/shard_map/while/body/eval_jaxpr/ppermute | solution.py:10
  65.7 1.2 slice-start
  72.8 19.5 %collective-permute-start = (bf16[128,1024]{0,1:T(8,128)(2,1)S(1)}, bf16[128,1024]{0,1:T(8,128)(2,1)S(1)}, u32[]{:S(2)}, u32[]{:S(2)}) collective-permute-start(bf16[128,1024]{0,1:T(8,128)(2,1)S(1)} %get-tuple-element.1186), channel_id=1, source_target_pairs={{0,2},{2,4},{4,6},{6,8},{8,10},{10,12},{12,14},{14,16},{16,18},{18... | collective-permute-start | bytes 786440 | tf_op jit(solution)/shard_map/while/body/eval_jaxpr/ppermute | solution.py:10
  76.2 16.7 %collective-permute-start.1 = (bf16[128,1024]{0,1:T(8,128)(2,1)}, bf16[128,1024]{0,1:T(8,128)(2,1)S(1)}, u32[]{:S(2)}, u32[]{:S(2)}) collective-permute-start(bf16[128,1024]{0,1:T(8,128)(2,1)} %get-tuple-element.1187), channel_id=1, source_target_pairs={{0,2},{2,4},{4,6},{6,8},{8,10},{10,12},{12,14},{14,16},{16,18},{18... | collective-permute-start | bytes 786440 | tf_op jit(solution)/shard_map/while/body/eval_jaxpr/ppermute | solution.py:10
  89.5 1.2 slice-start
  108.2 1.2 slice-start.3
  112.1 1.5 copy-start.5
  112.1 2.8 %copy-start.4 = (bf16[1,128,1024]{1,2,0:T(8,128)(2,1)S(1)}, bf16[1,128,1024]{1,2,0:T(8,128)(2,1)}, u32[]{:S(2)}) copy-start(bf16[1,128,1024]{1,2,0:T(8,128)(2,1)} %slice.141) | copy-start | bytes 786436
  128.5 31.0 %collective-permute-start.2 = (f32[128,1024]{0,1:T(8,128)}, f32[128,1024]{0,1:T(8,128)}, u32[]{:S(2)}, u32[]{:S(2)}) collective-permute-start(f32[128,1024]{0,1:T(8,128)} %get-tuple-element.1244), channel_id=1, source_target_pairs={{2,0},{4,2},{6,4},{8,6},{10,8},{12,10},{14,12},{16,14},{18,16},{20... | collective-permute-start | bytes 1572872 | tf_op jit(solution)/shard_map/while/body/eval_jaxpr/ppermute | solution.py:10
  129.8 31.8 %collective-permute-start.3 = (f32[128,1024]{0,1:T(8,128)}, f32[128,1024]{0,1:T(8,128)}, u32[]{:S(2)}, u32[]{:S(2)}) collective-permute-start(f32[128,1024]{0,1:T(8,128)} %get-tuple-element.1245), channel_id=1, source_target_pairs={{2,0},{4,2},{6,4},{8,6},{10,8},{12,10},{14,12},{16,14},{18,16},{20... | collective-permute-start | bytes 1572872 | tf_op jit(solution)/shard_map/while/body/eval_jaxpr/ppermute | solution.py:10
  141.0 1.2 slice-start.1
  157.6 1.8 copy-start.1
  157.6 1.8 copy-start.2
  157.6 1.9 copy-start
  159.5 4.0 %copy-start.3 = (f32[128,1024]{0,1:T(8,128)}, f32[128,1024]{0,1:T(8,128)S(1)}, u32[]{:S(2)}) copy-start(f32[128,1024]{0,1:T(8,128)S(1)} %bitcast_add_fusion.6) | copy-start | bytes 1572868 | tf_op jit(solution)/shard_map/while
  163.5 31.0 %collective-permute-start.2 = (f32[128,1024]{0,1:T(8,128)}, f32[128,1024]{0,1:T(8,128)}, u32[]{:S(2)}, u32[]{:S(2)}) collective-permute-start(f32[128,1024]{0,1:T(8,128)} %get-tuple-element.1244), channel_id=1, source_target_pairs={{2,0},{4,2},{6,4},{8,6},{10,8},{12,10},{14,12},{16,14},{18,16},{20... | collective-permute-start | bytes 1572872 | tf_op jit(solution)/shard_map/while/body/eval_jaxpr/ppermute | solution.py:10
  164.8 31.8 %collective-permute-start.3 = (f32[128,1024]{0,1:T(8,128)}, f32[128,1024]{0,1:T(8,128)}, u32[]{:S(2)}, u32[]{:S(2)}) collective-permute-start(f32[128,1024]{0,1:T(8,128)} %get-tuple-element.1245), channel_id=1, source_target_pairs={{2,0},{4,2},{6,4},{8,6},{10,8},{12,10},{14,12},{16,14},{18,16},{20... | collective-permute-start | bytes 1572872 | tf_op jit(solution)/shard_map/while/body/eval_jaxpr/ppermute | solution.py:10
  176.0 1.2 slice-start.1
  192.6 1.8 copy-start.1
  192.6 1.8 copy-start.2
  192.6 1.9 copy-start
  194.5 4.0 %copy-start.3 = (f32[128,1024]{0,1:T(8,128)}, f32[128,1024]{0,1:T(8,128)S(1)}, u32[]{:S(2)}) copy-start(f32[128,1024]{0,1:T(8,128)S(1)} %bitcast_add_fusion.6) | copy-start | bytes 1572868 | tf_op jit(solution)/shard_map/while
  198.5 31.0 %collective-permute-start.2 = (f32[128,1024]{0,1:T(8,128)}, f32[128,1024]{0,1:T(8,128)}, u32[]{:S(2)}, u32[]{:S(2)}) collective-permute-start(f32[128,1024]{0,1:T(8,128)} %get-tuple-element.1244), channel_id=1, source_target_pairs={{2,0},{4,2},{6,4},{8,6},{10,8},{12,10},{14,12},{16,14},{18,16},{20... | collective-permute-start | bytes 1572872 | tf_op jit(solution)/shard_map/while/body/eval_jaxpr/ppermute | solution.py:10
  199.7 31.8 %collective-permute-start.3 = (f32[128,1024]{0,1:T(8,128)}, f32[128,1024]{0,1:T(8,128)}, u32[]{:S(2)}, u32[]{:S(2)}) collective-permute-start(f32[128,1024]{0,1:T(8,128)} %get-tuple-element.1245), channel_id=1, source_target_pairs={{2,0},{4,2},{6,4},{8,6},{10,8},{12,10},{14,12},{16,14},{18,16},{20... | collective-permute-start | bytes 1572872 | tf_op jit(solution)/shard_map/while/body/eval_jaxpr/ppermute | solution.py:10
  210.9 1.2 slice-start.1
  227.5 1.8 copy-start.1
  227.5 1.8 copy-start.2
  227.5 1.9 copy-start
  229.4 4.0 %copy-start.3 = (f32[128,1024]{0,1:T(8,128)}, f32[128,1024]{0,1:T(8,128)S(1)}, u32[]{:S(2)}) copy-start(f32[128,1024]{0,1:T(8,128)S(1)} %bitcast_add_fusion.6) | copy-start | bytes 1572868 | tf_op jit(solution)/shard_map/while
  233.4 7.4 %collective-permute-start.4 = (f32[16,128]{1,0:T(8,128)S(1)}, f32[16,128]{1,0:T(8,128)S(1)}, u32[]{:S(2)}, u32[]{:S(2)}) collective-permute-start(f32[16,128]{1,0:T(8,128)S(1)} %get-tuple-element.814), channel_id=1, source_target_pairs={{0,2},{2,0},{4,6},{6,4},{8,10},{10,8},{12,14},{14,12},{16,18},{18,... | collective-permute-start | bytes 24584 | tf_op jit(solution)/shard_map/ppermute | solution.py:138
  240.8 5.1 %collective-permute-start.5 = (f32[16,128]{1,0:T(8,128)S(1)}, f32[16,128]{1,0:T(8,128)S(1)}, u32[]{:S(2)}, u32[]{:S(2)}) collective-permute-start(f32[16,128]{1,0:T(8,128)S(1)} %add.208), channel_id=1, source_target_pairs={{0,4},{2,6},{4,0},{6,2},{8,12},{10,14},{12,8},{14,10},{16,20},{18,... | collective-permute-start | bytes 24584 | tf_op jit(solution)/shard_map/ppermute | solution.py:138
  245.9 8.0 %collective-permute-start.6 = (f32[16,128]{1,0:T(8,128)S(1)}, f32[16,128]{1,0:T(8,128)S(1)}, u32[]{:S(2)}, u32[]{:S(2)}) collective-permute-start(f32[16,128]{1,0:T(8,128)S(1)} %add.209), channel_id=1, source_target_pairs={{0,8},{2,10},{4,12},{6,14},{8,0},{10,2},{12,4},{14,6},{16,24},{18,... | collective-permute-start | bytes 24584 | tf_op jit(solution)/shard_map/ppermute | solution.py:138
  253.9 10.1 %collective-permute-start.7 = (f32[16,128]{1,0:T(8,128)S(1)}, f32[16,128]{1,0:T(8,128)S(1)}, u32[]{:S(2)}, u32[]{:S(2)}) collective-permute-start(f32[16,128]{1,0:T(8,128)S(1)} %add.210), channel_id=1, source_target_pairs={{0,16},{2,18},{4,20},{6,22},{8,24},{10,26},{12,28},{14,30},{16,0},... | collective-permute-start | bytes 24584 | tf_op jit(solution)/shard_map/ppermute | solution.py:138
